TPU v7x, 32 devices: a whole 2x2x4 slice. The times are simulated.
32 devices in a mesh: section: 4 (over y, x), rows: 2 (over core), dp: 4 (over z).
Axes of the slice: x: 2, y: 2, z: 4, core: 2. Of those that a mesh axis runs over, the one named last changes fastest.
Arguments:
- images: bfloat16 [8, 48, 16, 384], P('dp', 'rows'), may hold values from -6 to 6
- cotangent: bfloat16 [8, 48, 16, 384], P('dp', 'rows'), may hold values from -6 to 6
- order: int32 [4, 2], P('dp'), may hold values from 0 to 1, each once within a row
- heights: int32 [8], P('dp'), may hold values from 12 to 48, as said below
- kernel: float32 [4, 49, 384], P('section'), may hold values from -0.875 to 0.875
- biases: float32 [4, 3, 384], P('section'), may hold values from -3 to 3
- gain: float32 [4, 384], P('section'), may hold values from 0.25 to 1.75
- scale: float32 [4, 384], P('section'), may hold values from 0.4 to 1.2
- up_weight: bfloat16 [4, 384, 1536], P('section'), may hold values from -0.3125 to 0.3125
- up_bias: float32 [4, 1536], P('section'), may hold values from -3 to 3
- down_weight: bfloat16 [4, 1536, 384], P('section'), may hold values from -0.15625 to 0.15625
Outputs:
- kernel_grad: bfloat16 [4, 49, 384], P('section')
- bias_grad: bfloat16 [4, 3, 384], P('section')
- gain_grad: bfloat16 [4, 384], P('section')
- scale_grad: bfloat16 [4, 384], P('section')
- up_weight_grad: bfloat16 [4, 384, 1536], P('section')
- up_bias_grad: bfloat16 [4, 1536], P('section')
- down_weight_grad: bfloat16 [4, 1536, 384], P('section')
Inputs may be any that keep to these rules, and one draw needn't show every extreme that they name: `order`: each row holds every number of 0 to 1 once. `heights`: some image has all 48 rows and some image has 12 rows.
All inputs are finite; a program needn't handle non-finite values.
Results may differ from a plain program's by a relative error of at most 0.015.
Values may be sent and summed in bfloat16 or wider, within the bound.
No kernel may reach another device: no remote copies, remote signals or barrier semaphores. Data moves between devices by JAX's collectives and lax.ppermute only.
A program may use at most 128 MiB of HBM per device.

v0:
```python
import math
import jax
import jax.numpy as jnp
from jax import lax
from jax.sharding import PartitionSpec as P

EPS = 1e-06
ROOT_HALF = 0.7071067811865476
INV_ROOT_TAU = 0.3989422804014327


def extended(block, sides, width):
    for axis, dim in sides:
        count = lax.axis_size(axis)
        forward = [(i, i + 1) for i in range(count - 1)]
        backward = [(target, source) for source, target in forward]
        low = lax.ppermute(
            lax.slice_in_dim(block, block.shape[dim] - width, None, axis=dim), axis, forward
        )
        high = lax.ppermute(lax.slice_in_dim(block, 0, width, axis=dim), axis, backward)
        block = jnp.concatenate([low, block, high], axis=dim)
    return block


def shifted(value, axis, steps):
    count = lax.axis_size(axis)
    leading, last = (max(0, -steps), min(count, count - steps))
    return lax.ppermute(value, axis, [(source, source + steps) for source in range(leading, last)])


def gelu_exact(values):
    return 0.5 * values * (1.0 + lax.erf(values * ROOT_HALF))


def gelu_slope(values):
    return (
        0.5 * (1.0 + lax.erf(values * ROOT_HALF))
        + values * jnp.exp(-0.5 * values * values) * INV_ROOT_TAU
    )


def widen_cols(padded):
    return jnp.pad(padded.astype(jnp.float32), ((0, 0), (3, 3), (0, 0)))


def block_forward(padded, row_mask, params):
    kern, biases, gain, scale, up_weight, up_bias, down_weight = params
    row_count = padded.shape[0] - 6
    col_count = padded.shape[1]
    channels = padded.shape[2]
    field = widen_cols(padded)
    inner = field[3:-3, 3:-3]
    conv = jnp.zeros((row_count, col_count, channels), jnp.float32)
    for i in range(7):
        for j in range(7):
            conv = conv + kern[i * 7 + j] * field[i : i + row_count, j : j + col_count]
    conv = conv + biases[0]
    centred = conv - jnp.mean(conv, axis=-1, keepdims=True)
    inv_std = lax.rsqrt(jnp.mean(centred * centred, axis=-1, keepdims=True) + EPS)
    normed = centred * inv_std
    features = (normed * gain + biases[1]).astype(jnp.bfloat16).reshape(-1, channels)
    hidden_pre = jnp.dot(features, up_weight, preferred_element_type=jnp.float32) + up_bias
    hidden = gelu_exact(hidden_pre).astype(jnp.bfloat16)
    branch = (jnp.dot(hidden, down_weight, preferred_element_type=jnp.float32) + biases[2]).reshape(
        row_count, col_count, channels
    )
    output = (row_mask * (inner + scale * branch)).astype(jnp.bfloat16)
    return (output, (padded, normed, inv_std, features, hidden_pre, branch))


def block_backward_first(grad_out, saved, row_mask, params):
    padded, normed, inv_std, features, hidden_pre, branch = saved
    kern, biases, gain, scale, up_weight, up_bias, down_weight = params
    channels = normed.shape[2]
    grad_res = row_mask * grad_out.astype(jnp.float32)
    scaled = scale * grad_res
    grad_scale = jnp.sum(branch * grad_res, axis=(0, 1))
    grad_bias_out = jnp.sum(scaled, axis=(0, 1))
    grad_branch = scaled.astype(jnp.bfloat16).reshape(-1, channels)
    hidden = gelu_exact(hidden_pre).astype(jnp.bfloat16)
    grad_down = lax.dot_general(
        hidden, grad_branch, (((0,), (0,)), ((), ())), preferred_element_type=jnp.float32
    )
    grad_hidden = lax.dot_general(
        grad_branch, down_weight, (((1,), (1,)), ((), ())), preferred_element_type=jnp.float32
    )
    grad_pre = grad_hidden * gelu_slope(hidden_pre)
    grad_up_bias = jnp.sum(grad_pre, axis=0)
    grad_pre_low = grad_pre.astype(jnp.bfloat16)
    grad_up = lax.dot_general(
        features, grad_pre_low, (((0,), (0,)), ((), ())), preferred_element_type=jnp.float32
    )
    grad_feat = lax.dot_general(
        grad_pre_low, up_weight, (((1,), (1,)), ((), ())), preferred_element_type=jnp.float32
    ).reshape(normed.shape)
    grad_gain = jnp.sum(grad_feat * normed, axis=(0, 1))
    grad_norm_bias = jnp.sum(grad_feat, axis=(0, 1))
    grad_normed = grad_feat * gain
    grad_conv = inv_std * (
        grad_normed
        - jnp.mean(grad_normed, axis=-1, keepdims=True)
        - normed * jnp.mean(grad_normed * normed, axis=-1, keepdims=True)
    )
    grad_conv_bias = jnp.sum(grad_conv, axis=(0, 1))
    small = (
        jnp.stack([grad_conv_bias, grad_norm_bias, grad_bias_out]),
        grad_gain[None],
        grad_scale[None],
        grad_up,
        grad_up_bias[None],
        grad_down,
    )
    return (grad_res, grad_conv, small)


def block_backward_second(grad_res, grad_conv, conv_padded, padded, row_mask, kern):
    row_count = grad_conv.shape[0]
    col_count = grad_conv.shape[1]
    field = widen_cols(padded)
    spread = widen_cols(conv_padded)
    taps = []
    total = jnp.zeros(grad_conv.shape, jnp.float32)
    for i in range(7):
        for j in range(7):
            taps.append(
                jnp.sum(field[i : i + row_count, j : j + col_count] * grad_conv, axis=(0, 1))
            )
            total = (
                total
                + kern[i * 7 + j] * spread[6 - i : 6 - i + row_count, 6 - j : 6 - j + col_count]
            )
    grad_in = (row_mask * (grad_res + total)).astype(jnp.bfloat16)
    return (grad_in, jnp.stack(taps))


def body(
    images, cotangent, order, heights, kernel, biases, gain, scale, up_weight, up_bias, down_weight
):
    section_count = lax.axis_size("section")
    section_at = lax.axis_index("section")
    slot_count, row_count, col_count, channels = images.shape
    hidden_count = up_weight.shape[2]
    first_row = lax.axis_index("rows") * row_count
    lines = first_row + jnp.arange(row_count, dtype=jnp.int32)
    params = (kernel[0], biases[0], gain[0], scale[0], up_weight[0], up_bias[0], down_weight[0])
    tick_list = jnp.arange(slot_count + section_count - 1, dtype=jnp.int32)

    def slot_state(tick_no, lag):
        offset = tick_no - lag
        active = (offset >= 0) & (offset < slot_count)
        slot_at = jnp.clip(offset, 0, slot_count - 1)
        image_at = order[0, slot_at]
        height = heights[image_at]
        row_mask = (lines < height).astype(jnp.float32)[:, None, None]
        has_rows = active & (first_row < height)
        return (slot_at, image_at, row_mask, active, has_rows)

    store_start = (
        jnp.zeros((slot_count, row_count + 6, col_count, channels), jnp.bfloat16),
        jnp.zeros((slot_count, row_count, col_count, channels), jnp.float32),
        jnp.zeros((slot_count, row_count, col_count, 1), jnp.float32),
        jnp.zeros((slot_count, row_count * col_count, channels), jnp.bfloat16),
        jnp.zeros((slot_count, row_count * col_count, hidden_count), jnp.float32),
        jnp.zeros((slot_count, row_count, col_count, channels), jnp.float32),
    )

    def forward_tick(carry, tick_no):
        incoming, stored = carry
        slot_at, image_at, row_mask, active, has_rows = slot_state(tick_no, section_at)
        fresh = jnp.where(row_mask > 0, images[image_at], jnp.zeros((), jnp.bfloat16))
        entering = jnp.where(section_at == 0, fresh, incoming)
        padded = extended(entering, (("rows", 0),), 3)
        result, saved = block_forward(padded, row_mask, params)
        stored = tuple(
            (
                whole.at[slot_at].set(jnp.where(active, piece, whole[slot_at]))
                for whole, piece in zip(stored, saved)
            )
        )
        outgoing = shifted(result, "section", 1)
        return ((outgoing, stored), None)

    blank_act = jnp.zeros((row_count, col_count, channels), jnp.bfloat16)
    stored = lax.scan(forward_tick, (blank_act, store_start), tick_list)[0][1]

    def backward_tick(carry, tick_no):
        incoming, totals = carry
        slot_at, image_at, row_mask, active, has_rows = slot_state(
            tick_no, section_count - 1 - section_at
        )
        grad_out = jnp.where(section_at == section_count - 1, cotangent[slot_at], incoming)
        saved = tuple((whole[slot_at] for whole in stored))
        grad_res, grad_conv, small = block_backward_first(grad_out, saved, row_mask, params)
        conv_padded = extended(grad_conv.astype(jnp.bfloat16), (("rows", 0),), 3).astype(
            grad_conv.dtype
        )
        grad_in, taps = block_backward_second(
            grad_res, grad_conv, conv_padded, saved[0], row_mask, params[0]
        )
        terms = (taps,) + small
        totals = tuple((total + jnp.where(active, term, 0.0) for total, term in zip(totals, terms)))
        outgoing = shifted(grad_in, "section", -1)
        return ((outgoing, totals), None)

    grads_start = (
        jnp.zeros((49, channels), jnp.float32),
        jnp.zeros((3, channels), jnp.float32),
        jnp.zeros((1, channels), jnp.float32),
        jnp.zeros((1, channels), jnp.float32),
        jnp.zeros((channels, hidden_count), jnp.float32),
        jnp.zeros((1, hidden_count), jnp.float32),
        jnp.zeros((hidden_count, channels), jnp.float32),
    )
    totals = lax.scan(backward_tick, (blank_act, grads_start), tick_list)[0][1]
    factor = 1.0 / math.sqrt(
        lax.axis_size("dp") * slot_count * lax.axis_size("rows") * row_count * col_count
    )
    summed = lax.psum(
        (totals[0], totals[1], totals[2], totals[3], totals[4], totals[5], totals[6]),
        ("rows", "dp"),
    )
    finished = tuple(((part * factor).astype(jnp.bfloat16) for part in summed))
    return (
        finished[0][None],
        finished[1][None],
        finished[2],
        finished[3],
        finished[4][None],
        finished[5],
        finished[6][None],
    )


def solution(mesh):
    in_specs = (
        P("dp", "rows", None, None),
        P("dp", "rows", None, None),
        P("dp", None),
        P("dp"),
        P("section", None, None),
        P("section", None, None),
        P("section", None),
        P("section", None),
        P("section", None, None),
        P("section", None),
        P("section", None, None),
    )
    out_specs = (
        P("section", None, None),
        P("section", None, None),
        P("section", None),
        P("section", None),
        P("section", None, None),
        P("section", None),
        P("section", None, None),
    )
    return jax.shard_map(body, mesh=mesh, in_specs=in_specs, out_specs=out_specs, check_vma=False)
```

profile of v0, /device:TPU:0, one launch (start us, length us, event | category | flops | bytes accessed | tf_op | source)
XLA Modules:
  0.0 707.3 jit_solution(5315911890575509953)
XLA Ops:
  10.1 2.7 broadcast_in_dim.122
  17.4 230.1 %while.58 = (s32[]{:T(128)}, bf16[24,16,384]{2,1,0:T(8,128)(2,1)S(1)}, bf16[2,30,16,384]{3,2,1,0:T(8,128)(2,1)}, f32[2,24,16,384]{3,2,1,0:T(8,128)}, f32[2,24,16...) while((s32[]{:T(128)}, ...), condition=%wide.region_5.6_spmd.clone, body=%wide.region_0.5_spmd.clone.sunk | while | flops 930707456 | bytes 118534944 | solution.py:184
  26.7 3.0 collective-permute-start.1
  42.0 5.4 fusion.394
  52.5 5.1 collective-permute-start.2
  61.0 2.4 collective-permute-done.2
  72.7 3.0 collective-permute-start.1
  88.0 5.4 fusion.394
  98.6 4.7 collective-permute-start.2
  118.3 3.0 collective-permute-start.1
  133.6 5.4 fusion.394
  144.2 4.7 collective-permute-start.2
  163.9 3.0 collective-permute-start.1
  179.2 5.4 fusion.394
  189.8 5.5 collective-permute-start.2
  198.6 2.4 collective-permute-done.2
  210.3 3.0 collective-permute-start.1
  225.6 5.4 fusion.394
  236.1 5.6 collective-permute-start.2
  245.1 2.4 collective-permute-done.2
  248.1 328.2 %while.59 = (s32[]{:T(128)}, bf16[24,16,384]{2,1,0:T(8,128)(2,1)S(1)}, f32[49,384]{1,0:T(8,128)}, f32[3,384]{1,0:T(4,128)}, f32[1,384]{1,0:T(1,128)}, /*index=5*...) while((s32[]{:T(128)}, ...), condition=%wide.region_64.65_spmd.clone, body=%wide.region_6.64_spmd.clone.sunk | while | flops 1859761920 | bytes 116535416 | solution.py:214
  258.3 3.3 fusion.410
  272.6 4.2 collective-permute-start.4
  285.7 3.4 fusion.423
  293.4 5.0 fusion.416
  323.0 3.3 fusion.410
  330.1 2.4 fusion.413
  337.3 4.2 collective-permute-start.4
  350.5 3.4 fusion.423
  358.2 5.0 fusion.416
  388.5 3.3 fusion.410
  395.6 2.4 fusion.413
  402.8 4.2 collective-permute-start.4
  416.0 3.4 fusion.423
  423.7 5.0 fusion.416
  454.0 3.3 fusion.410
  461.0 2.4 fusion.413
  468.3 4.2 collective-permute-start.4
  482.1 3.4 fusion.423
  489.8 5.0 fusion.416
  520.1 3.3 fusion.410
  527.2 2.4 fusion.413
  534.4 4.2 collective-permute-start.4
  548.2 3.4 fusion.423
  555.9 5.0 fusion.416
  577.0 28.8 %all-reduce.3 = (f32[3,384]{1,0:T(4,128)S(1)}, f32[1,384]{1,0:T(1,128)S(1)}, f32[1,384]{1,0:T(1,128)S(1)}, f32[1,1536]{1,0:T(1,128)S(1)}) all-reduce(f32[3,384]{1,0:T(4,128)S(1)} %copy-done.39, f32[1,384]{1,0:T(1,128)S(1)} %copy-done.90, f32[1,384]{1,0:T(1,128)S(1)} %copy-done.91, ...), channel_id=1, replica_groups=mesh['section'=4,'rows'=2,'dp'=4] {'rows','dp'}, use_global_device_ids=true, to_apply=%region_66.67 | all-reduce | flops 3456 | bytes 27648 | tf_op jit(solution)/shard_map/psum | solution.py:218
  607.6 88.0 %all-reduce.7.cloned.1.call-done = (f32[49,384]{1,0:T(8,128)}, f32[384,1536]{1,0:T(8,128)}, f32[1536,384]{1,0:T(8,128)}) async-done(((f32[49,384]{1,0:T(8,128)}, f32[384,1536]{1,0:T(8,128)}, f32[1536,384]{1,0:T(8,128)}), (f32[49,384]{1,0:T(8,128)}, f32[384,1536]{1,0:T(8,128)}, f32[1536,384]{1,0:T(8,128)})) %all-reduce.7.cloned.1.call-update) | async-done | bytes 4793872 | tf_op jit(solution)/shard_map/psum | solution.py:218
  695.6 3.0 fusion.334
  (1600 shorter events, 371.3 us)
Async XLA Ops:
  7.2 688.4 %all-reduce.7.cloned.1.call-start = ((), (), s32[]{:S(2)}) async-start(), calls=%async_computation | async-start | bytes 9609216 | tf_op jit(solution)/shard_map/psum | solution.py:218
  25.4 16.5 %collective-permute-start = (bf16[3,16,384]{2,1,0:T(8,128)(2,1)S(1)}, bf16[3,16,384]{2,1,0:T(8,128)(2,1)S(1)}, u32[]{:S(2)}, u32[]{:S(2)}) collective-permute-start(bf16[3,16,384]{2,1,0:T(8,128)(2,1)S(1)} %get-tuple-element.1573), channel_id=1, source_target_pairs={{4,0},{5,1},{6,2},{7,3},{12,8},{13,9},{14,10},{15,11},{20,16},{21,... | collective-permute-start | bytes 110600 | tf_op jit(solution)/shard_map/while/body/eval_jaxpr/ppermute | solution.py:20
  26.7 15.2 %collective-permute-start.1 = (bf16[3,16,384]{2,1,0:T(8,128)(2,1)S(1)}, bf16[3,16,384]{2,1,0:T(8,128)(2,1)S(1)}, u32[]{:S(2)}, u32[]{:S(2)}) collective-permute-start(bf16[3,16,384]{2,1,0:T(8,128)(2,1)S(1)} %get-tuple-element.1574), channel_id=1, source_target_pairs={{0,4},{1,5},{2,6},{3,7},{8,12},{9,13},{10,14},{11,15},{16,20},{17,... | collective-permute-start | bytes 110600 | tf_op jit(solution)/shard_map/while/body/eval_jaxpr/ppermute | solution.py:17
  52.5 10.9 %collective-permute-start.2 = (bf16[24,16,384]{2,1,0:T(8,128)(2,1)S(1)}, bf16[24,16,384]{2,1,0:T(8,128)(2,1)S(1)}, u32[]{:S(2)}, u32[]{:S(2)}) collective-permute-start(bf16[24,16,384]{2,1,0:T(8,128)(2,1)S(1)} %multiply_convert_fusion.15), channel_id=1, source_target_pairs={{0,8},{8,16},{16,24},{1,9},{9,17},{17,25},{2,10},{10,18},{18,26},{... | collective-permute-start | bytes 884744 | tf_op jit(solution)/shard_map/while/body/eval_jaxpr/ppermute | solution.py:28
  71.4 16.5 %collective-permute-start = (bf16[3,16,384]{2,1,0:T(8,128)(2,1)S(1)}, bf16[3,16,384]{2,1,0:T(8,128)(2,1)S(1)}, u32[]{:S(2)}, u32[]{:S(2)}) collective-permute-start(bf16[3,16,384]{2,1,0:T(8,128)(2,1)S(1)} %get-tuple-element.1573), channel_id=1, source_target_pairs={{4,0},{5,1},{6,2},{7,3},{12,8},{13,9},{14,10},{15,11},{20,16},{21,... | collective-permute-start | bytes 110600 | tf_op jit(solution)/shard_map/while/body/eval_jaxpr/ppermute | solution.py:20
  72.7 15.2 %collective-permute-start.1 = (bf16[3,16,384]{2,1,0:T(8,128)(2,1)S(1)}, bf16[3,16,384]{2,1,0:T(8,128)(2,1)S(1)}, u32[]{:S(2)}, u32[]{:S(2)}) collective-permute-start(bf16[3,16,384]{2,1,0:T(8,128)(2,1)S(1)} %get-tuple-element.1574), channel_id=1, source_target_pairs={{0,4},{1,5},{2,6},{3,7},{8,12},{9,13},{10,14},{11,15},{16,20},{17,... | collective-permute-start | bytes 110600 | tf_op jit(solution)/shard_map/while/body/eval_jaxpr/ppermute | solution.py:17
  98.6 10.5 %collective-permute-start.2 = (bf16[24,16,384]{2,1,0:T(8,128)(2,1)S(1)}, bf16[24,16,384]{2,1,0:T(8,128)(2,1)S(1)}, u32[]{:S(2)}, u32[]{:S(2)}) collective-permute-start(bf16[24,16,384]{2,1,0:T(8,128)(2,1)S(1)} %multiply_convert_fusion.15), channel_id=1, source_target_pairs={{0,8},{8,16},{16,24},{1,9},{9,17},{17,25},{2,10},{10,18},{18,26},{... | collective-permute-start | bytes 884744 | tf_op jit(solution)/shard_map/while/body/eval_jaxpr/ppermute | solution.py:28
  117.0 16.5 %collective-permute-start = (bf16[3,16,384]{2,1,0:T(8,128)(2,1)S(1)}, bf16[3,16,384]{2,1,0:T(8,128)(2,1)S(1)}, u32[]{:S(2)}, u32[]{:S(2)}) collective-permute-start(bf16[3,16,384]{2,1,0:T(8,128)(2,1)S(1)} %get-tuple-element.1573), channel_id=1, source_target_pairs={{4,0},{5,1},{6,2},{7,3},{12,8},{13,9},{14,10},{15,11},{20,16},{21,... | collective-permute-start | bytes 110600 | tf_op jit(solution)/shard_map/while/body/eval_jaxpr/ppermute | solution.py:20
  118.3 15.2 %collective-permute-start.1 = (bf16[3,16,384]{2,1,0:T(8,128)(2,1)S(1)}, bf16[3,16,384]{2,1,0:T(8,128)(2,1)S(1)}, u32[]{:S(2)}, u32[]{:S(2)}) collective-permute-start(bf16[3,16,384]{2,1,0:T(8,128)(2,1)S(1)} %get-tuple-element.1574), channel_id=1, source_target_pairs={{0,4},{1,5},{2,6},{3,7},{8,12},{9,13},{10,14},{11,15},{16,20},{17,... | collective-permute-start | bytes 110600 | tf_op jit(solution)/shard_map/while/body/eval_jaxpr/ppermute | solution.py:17
  144.2 10.5 %collective-permute-start.2 = (bf16[24,16,384]{2,1,0:T(8,128)(2,1)S(1)}, bf16[24,16,384]{2,1,0:T(8,128)(2,1)S(1)}, u32[]{:S(2)}, u32[]{:S(2)}) collective-permute-start(bf16[24,16,384]{2,1,0:T(8,128)(2,1)S(1)} %multiply_convert_fusion.15), channel_id=1, source_target_pairs={{0,8},{8,16},{16,24},{1,9},{9,17},{17,25},{2,10},{10,18},{18,26},{... | collective-permute-start | bytes 884744 | tf_op jit(solution)/shard_map/while/body/eval_jaxpr/ppermute | solution.py:28
  162.6 16.5 %collective-permute-start = (bf16[3,16,384]{2,1,0:T(8,128)(2,1)S(1)}, bf16[3,16,384]{2,1,0:T(8,128)(2,1)S(1)}, u32[]{:S(2)}, u32[]{:S(2)}) collective-permute-start(bf16[3,16,384]{2,1,0:T(8,128)(2,1)S(1)} %get-tuple-element.1573), channel_id=1, source_target_pairs={{4,0},{5,1},{6,2},{7,3},{12,8},{13,9},{14,10},{15,11},{20,16},{21,... | collective-permute-start | bytes 110600 | tf_op jit(solution)/shard_map/while/body/eval_jaxpr/ppermute | solution.py:20
  163.9 15.2 %collective-permute-start.1 = (bf16[3,16,384]{2,1,0:T(8,128)(2,1)S(1)}, bf16[3,16,384]{2,1,0:T(8,128)(2,1)S(1)}, u32[]{:S(2)}, u32[]{:S(2)}) collective-permute-start(bf16[3,16,384]{2,1,0:T(8,128)(2,1)S(1)} %get-tuple-element.1574), channel_id=1, source_target_pairs={{0,4},{1,5},{2,6},{3,7},{8,12},{9,13},{10,14},{11,15},{16,20},{17,... | collective-permute-start | bytes 110600 | tf_op jit(solution)/shard_map/while/body/eval_jaxpr/ppermute | solution.py:17
  189.8 11.3 %collective-permute-start.2 = (bf16[24,16,384]{2,1,0:T(8,128)(2,1)S(1)}, bf16[24,16,384]{2,1,0:T(8,128)(2,1)S(1)}, u32[]{:S(2)}, u32[]{:S(2)}) collective-permute-start(bf16[24,16,384]{2,1,0:T(8,128)(2,1)S(1)} %multiply_convert_fusion.15), channel_id=1, source_target_pairs={{0,8},{8,16},{16,24},{1,9},{9,17},{17,25},{2,10},{10,18},{18,26},{... | collective-permute-start | bytes 884744 | tf_op jit(solution)/shard_map/while/body/eval_jaxpr/ppermute | solution.py:28
  209.0 16.5 %collective-permute-start = (bf16[3,16,384]{2,1,0:T(8,128)(2,1)S(1)}, bf16[3,16,384]{2,1,0:T(8,128)(2,1)S(1)}, u32[]{:S(2)}, u32[]{:S(2)}) collective-permute-start(bf16[3,16,384]{2,1,0:T(8,128)(2,1)S(1)} %get-tuple-element.1573), channel_id=1, source_target_pairs={{4,0},{5,1},{6,2},{7,3},{12,8},{13,9},{14,10},{15,11},{20,16},{21,... | collective-permute-start | bytes 110600 | tf_op jit(solution)/shard_map/while/body/eval_jaxpr/ppermute | solution.py:20
  210.3 15.2 %collective-permute-start.1 = (bf16[3,16,384]{2,1,0:T(8,128)(2,1)S(1)}, bf16[3,16,384]{2,1,0:T(8,128)(2,1)S(1)}, u32[]{:S(2)}, u32[]{:S(2)}) collective-permute-start(bf16[3,16,384]{2,1,0:T(8,128)(2,1)S(1)} %get-tuple-element.1574), channel_id=1, source_target_pairs={{0,4},{1,5},{2,6},{3,7},{8,12},{9,13},{10,14},{11,15},{16,20},{17,... | collective-permute-start | bytes 110600 | tf_op jit(solution)/shard_map/while/body/eval_jaxpr/ppermute | solution.py:17
  236.1 11.4 %collective-permute-start.2 = (bf16[24,16,384]{2,1,0:T(8,128)(2,1)S(1)}, bf16[24,16,384]{2,1,0:T(8,128)(2,1)S(1)}, u32[]{:S(2)}, u32[]{:S(2)}) collective-permute-start(bf16[24,16,384]{2,1,0:T(8,128)(2,1)S(1)} %multiply_convert_fusion.15), channel_id=1, source_target_pairs={{0,8},{8,16},{16,24},{1,9},{9,17},{17,25},{2,10},{10,18},{18,26},{... | collective-permute-start | bytes 884744 | tf_op jit(solution)/shard_map/while/body/eval_jaxpr/ppermute | solution.py:28
  248.3 9.9 %copy-start.87 = (f32[1,384]{1,0:T(1,128)S(1)}, f32[1,384]{1,0:T(1,128)}, u32[]{:S(2)}) copy-start(f32[1,384]{1,0:T(1,128)} %get-tuple-element.1945) | copy-start | bytes 4612 | tf_op jit(solution)/shard_map/while
  248.3 9.9 %copy-start.97 = (bf16[1536,384]{1,0:T(8,128)(2,1)S(1)}, bf16[1536,384]{1,0:T(8,128)(2,1)}, u32[]{:S(2)}) copy-start(bf16[1536,384]{1,0:T(8,128)(2,1)} %get-tuple-element.1942) | copy-start | bytes 3538948 | tf_op jit(solution)/shard_map/while
  271.3 20.9 %collective-permute-start.3 = (bf16[3,16,384]{2,1,0:T(8,128)(2,1)}, bf16[3,16,384]{2,1,0:T(8,128)(2,1)}, u32[]{:S(2)}, u32[]{:S(2)}) collective-permute-start(bf16[3,16,384]{2,1,0:T(8,128)(2,1)} %get-tuple-element.1666), channel_id=1, source_target_pairs={{4,0},{5,1},{6,2},{7,3},{12,8},{13,9},{14,10},{15,11},{20,16},{21,... | collective-permute-start | bytes 110600 | tf_op jit(solution)/shard_map/while/body/eval_jaxpr/ppermute | solution.py:20
  272.6 19.6 %collective-permute-start.4 = (bf16[3,16,384]{2,1,0:T(8,128)(2,1)}, bf16[3,16,384]{2,1,0:T(8,128)(2,1)}, u32[]{:S(2)}, u32[]{:S(2)}) collective-permute-start(bf16[3,16,384]{2,1,0:T(8,128)(2,1)} %get-tuple-element.1667), channel_id=1, source_target_pairs={{0,4},{1,5},{2,6},{3,7},{8,12},{9,13},{10,14},{11,15},{16,20},{17,... | collective-permute-start | bytes 110600 | tf_op jit(solution)/shard_map/while/body/eval_jaxpr/ppermute | solution.py:17
  293.4 18.8 %copy-start.85 = (f32[384]{0:T(512)S(1)}, f32[384]{0:T(512)}, u32[]{:S(2)}) copy-start(f32[384]{0:T(512)} %get-tuple-element.1766) | copy-start | bytes 4612 | tf_op jit(solution)/shard_map/while
  293.4 19.0 %copy-start.27 = (f32[49,384]{1,0:T(8,128)S(1)}, f32[49,384]{1,0:T(8,128)}, u32[]{:S(2)}) copy-start(f32[49,384]{1,0:T(8,128)} %get-tuple-element.1895) | copy-start | bytes 225796 | tf_op jit(solution)/shard_map/while
  298.5 14.0 %collective-permute-start.5 = (bf16[24,16,384]{2,1,0:T(8,128)(2,1)S(1)}, bf16[24,16,384]{2,1,0:T(8,128)(2,1)S(1)}, u32[]{:S(2)}, u32[]{:S(2)}) collective-permute-start(bf16[24,16,384]{2,1,0:T(8,128)(2,1)S(1)} %fusion.416), channel_id=1, source_target_pairs={{8,0},{16,8},{24,16},{9,1},{17,9},{25,17},{10,2},{18,10},{26,18},{... | collective-permute-start | bytes 884744 | tf_op jit(solution)/shard_map/while/body/eval_jaxpr/ppermute | solution.py:28
  313.1 9.9 %copy-start.87 = (f32[1,384]{1,0:T(1,128)S(1)}, f32[1,384]{1,0:T(1,128)}, u32[]{:S(2)}) copy-start(f32[1,384]{1,0:T(1,128)} %get-tuple-element.1945) | copy-start | bytes 4612 | tf_op jit(solution)/shard_map/while
  313.1 9.9 %copy-start.97 = (bf16[1536,384]{1,0:T(8,128)(2,1)S(1)}, bf16[1536,384]{1,0:T(8,128)(2,1)}, u32[]{:S(2)}) copy-start(bf16[1536,384]{1,0:T(8,128)(2,1)} %get-tuple-element.1942) | copy-start | bytes 3538948 | tf_op jit(solution)/shard_map/while
  336.1 20.9 %collective-permute-start.3 = (bf16[3,16,384]{2,1,0:T(8,128)(2,1)}, bf16[3,16,384]{2,1,0:T(8,128)(2,1)}, u32[]{:S(2)}, u32[]{:S(2)}) collective-permute-start(bf16[3,16,384]{2,1,0:T(8,128)(2,1)} %get-tuple-element.1666), channel_id=1, source_target_pairs={{4,0},{5,1},{6,2},{7,3},{12,8},{13,9},{14,10},{15,11},{20,16},{21,... | collective-permute-start | bytes 110600 | tf_op jit(solution)/shard_map/while/body/eval_jaxpr/ppermute | solution.py:20
  337.3 19.6 %collective-permute-start.4 = (bf16[3,16,384]{2,1,0:T(8,128)(2,1)}, bf16[3,16,384]{2,1,0:T(8,128)(2,1)}, u32[]{:S(2)}, u32[]{:S(2)}) collective-permute-start(bf16[3,16,384]{2,1,0:T(8,128)(2,1)} %get-tuple-element.1667), channel_id=1, source_target_pairs={{0,4},{1,5},{2,6},{3,7},{8,12},{9,13},{10,14},{11,15},{16,20},{17,... | collective-permute-start | bytes 110600 | tf_op jit(solution)/shard_map/while/body/eval_jaxpr/ppermute | solution.py:17
  358.2 19.5 %copy-start.85 = (f32[384]{0:T(512)S(1)}, f32[384]{0:T(512)}, u32[]{:S(2)}) copy-start(f32[384]{0:T(512)} %get-tuple-element.1766) | copy-start | bytes 4612 | tf_op jit(solution)/shard_map/while
  358.2 19.7 %copy-start.27 = (f32[49,384]{1,0:T(8,128)S(1)}, f32[49,384]{1,0:T(8,128)}, u32[]{:S(2)}) copy-start(f32[49,384]{1,0:T(8,128)} %get-tuple-element.1895) | copy-start | bytes 225796 | tf_op jit(solution)/shard_map/while
  363.3 14.7 %collective-permute-start.5 = (bf16[24,16,384]{2,1,0:T(8,128)(2,1)S(1)}, bf16[24,16,384]{2,1,0:T(8,128)(2,1)S(1)}, u32[]{:S(2)}, u32[]{:S(2)}) collective-permute-start(bf16[24,16,384]{2,1,0:T(8,128)(2,1)S(1)} %fusion.416), channel_id=1, source_target_pairs={{8,0},{16,8},{24,16},{9,1},{17,9},{25,17},{10,2},{18,10},{26,18},{... | collective-permute-start | bytes 884744 | tf_op jit(solution)/shard_map/while/body/eval_jaxpr/ppermute | solution.py:28
  378.6 9.9 %copy-start.97 = (bf16[1536,384]{1,0:T(8,128)(2,1)S(1)}, bf16[1536,384]{1,0:T(8,128)(2,1)}, u32[]{:S(2)}) copy-start(bf16[1536,384]{1,0:T(8,128)(2,1)} %get-tuple-element.1942) | copy-start | bytes 3538948 | tf_op jit(solution)/shard_map/while
  401.5 20.9 %collective-permute-start.3 = (bf16[3,16,384]{2,1,0:T(8,128)(2,1)}, bf16[3,16,384]{2,1,0:T(8,128)(2,1)}, u32[]{:S(2)}, u32[]{:S(2)}) collective-permute-start(bf16[3,16,384]{2,1,0:T(8,128)(2,1)} %get-tuple-element.1666), channel_id=1, source_target_pairs={{4,0},{5,1},{6,2},{7,3},{12,8},{13,9},{14,10},{15,11},{20,16},{21,... | collective-permute-start | bytes 110600 | tf_op jit(solution)/shard_map/while/body/eval_jaxpr/ppermute | solution.py:20
  402.8 19.6 %collective-permute-start.4 = (bf16[3,16,384]{2,1,0:T(8,128)(2,1)}, bf16[3,16,384]{2,1,0:T(8,128)(2,1)}, u32[]{:S(2)}, u32[]{:S(2)}) collective-permute-start(bf16[3,16,384]{2,1,0:T(8,128)(2,1)} %get-tuple-element.1667), channel_id=1, source_target_pairs={{0,4},{1,5},{2,6},{3,7},{8,12},{9,13},{10,14},{11,15},{16,20},{17,... | collective-permute-start | bytes 110600 | tf_op jit(solution)/shard_map/while/body/eval_jaxpr/ppermute | solution.py:17
  423.7 19.5 %copy-start.85 = (f32[384]{0:T(512)S(1)}, f32[384]{0:T(512)}, u32[]{:S(2)}) copy-start(f32[384]{0:T(512)} %get-tuple-element.1766) | copy-start | bytes 4612 | tf_op jit(solution)/shard_map/while
  423.7 19.7 %copy-start.27 = (f32[49,384]{1,0:T(8,128)S(1)}, f32[49,384]{1,0:T(8,128)}, u32[]{:S(2)}) copy-start(f32[49,384]{1,0:T(8,128)} %get-tuple-element.1895) | copy-start | bytes 225796 | tf_op jit(solution)/shard_map/while
  428.7 14.7 %collective-permute-start.5 = (bf16[24,16,384]{2,1,0:T(8,128)(2,1)S(1)}, bf16[24,16,384]{2,1,0:T(8,128)(2,1)S(1)}, u32[]{:S(2)}, u32[]{:S(2)}) collective-permute-start(bf16[24,16,384]{2,1,0:T(8,128)(2,1)S(1)} %fusion.416), channel_id=1, source_target_pairs={{8,0},{16,8},{24,16},{9,1},{17,9},{25,17},{10,2},{18,10},{26,18},{... | collective-permute-start | bytes 884744 | tf_op jit(solution)/shard_map/while/body/eval_jaxpr/ppermute | solution.py:28
  444.1 9.9 %copy-start.97 = (bf16[1536,384]{1,0:T(8,128)(2,1)S(1)}, bf16[1536,384]{1,0:T(8,128)(2,1)}, u32[]{:S(2)}) copy-start(bf16[1536,384]{1,0:T(8,128)(2,1)} %get-tuple-element.1942) | copy-start | bytes 3538948 | tf_op jit(solution)/shard_map/while
  467.0 21.5 %collective-permute-start.3 = (bf16[3,16,384]{2,1,0:T(8,128)(2,1)}, bf16[3,16,384]{2,1,0:T(8,128)(2,1)}, u32[]{:S(2)}, u32[]{:S(2)}) collective-permute-start(bf16[3,16,384]{2,1,0:T(8,128)(2,1)} %get-tuple-element.1666), channel_id=1, source_target_pairs={{4,0},{5,1},{6,2},{7,3},{12,8},{13,9},{14,10},{15,11},{20,16},{21,... | collective-permute-start | bytes 110600 | tf_op jit(solution)/shard_map/while/body/eval_jaxpr/ppermute | solution.py:20
  468.3 20.2 %collective-permute-start.4 = (bf16[3,16,384]{2,1,0:T(8,128)(2,1)}, bf16[3,16,384]{2,1,0:T(8,128)(2,1)}, u32[]{:S(2)}, u32[]{:S(2)}) collective-permute-start(bf16[3,16,384]{2,1,0:T(8,128)(2,1)} %get-tuple-element.1667), channel_id=1, source_target_pairs={{0,4},{1,5},{2,6},{3,7},{8,12},{9,13},{10,14},{11,15},{16,20},{17,... | collective-permute-start | bytes 110600 | tf_op jit(solution)/shard_map/while/body/eval_jaxpr/ppermute | solution.py:17
  489.8 19.5 %copy-start.85 = (f32[384]{0:T(512)S(1)}, f32[384]{0:T(512)}, u32[]{:S(2)}) copy-start(f32[384]{0:T(512)} %get-tuple-element.1766) | copy-start | bytes 4612 | tf_op jit(solution)/shard_map/while
  489.8 19.7 %copy-start.27 = (f32[49,384]{1,0:T(8,128)S(1)}, f32[49,384]{1,0:T(8,128)}, u32[]{:S(2)}) copy-start(f32[49,384]{1,0:T(8,128)} %get-tuple-element.1895) | copy-start | bytes 225796 | tf_op jit(solution)/shard_map/while
  494.9 14.7 %collective-permute-start.5 = (bf16[24,16,384]{2,1,0:T(8,128)(2,1)S(1)}, bf16[24,16,384]{2,1,0:T(8,128)(2,1)S(1)}, u32[]{:S(2)}, u32[]{:S(2)}) collective-permute-start(bf16[24,16,384]{2,1,0:T(8,128)(2,1)S(1)} %fusion.416), channel_id=1, source_target_pairs={{8,0},{16,8},{24,16},{9,1},{17,9},{25,17},{10,2},{18,10},{26,18},{... | collective-permute-start | bytes 884744 | tf_op jit(solution)/shard_map/while/body/eval_jaxpr/ppermute | solution.py:28
  510.2 9.9 %copy-start.97 = (bf16[1536,384]{1,0:T(8,128)(2,1)S(1)}, bf16[1536,384]{1,0:T(8,128)(2,1)}, u32[]{:S(2)}) copy-start(bf16[1536,384]{1,0:T(8,128)(2,1)} %get-tuple-element.1942) | copy-start | bytes 3538948 | tf_op jit(solution)/shard_map/while
  533.1 21.5 %collective-permute-start.3 = (bf16[3,16,384]{2,1,0:T(8,128)(2,1)}, bf16[3,16,384]{2,1,0:T(8,128)(2,1)}, u32[]{:S(2)}, u32[]{:S(2)}) collective-permute-start(bf16[3,16,384]{2,1,0:T(8,128)(2,1)} %get-tuple-element.1666), channel_id=1, source_target_pairs={{4,0},{5,1},{6,2},{7,3},{12,8},{13,9},{14,10},{15,11},{20,16},{21,... | collective-permute-start | bytes 110600 | tf_op jit(solution)/shard_map/while/body/eval_jaxpr/ppermute | solution.py:20
  534.4 20.2 %collective-permute-start.4 = (bf16[3,16,384]{2,1,0:T(8,128)(2,1)}, bf16[3,16,384]{2,1,0:T(8,128)(2,1)}, u32[]{:S(2)}, u32[]{:S(2)}) collective-permute-start(bf16[3,16,384]{2,1,0:T(8,128)(2,1)} %get-tuple-element.1667), channel_id=1, source_target_pairs={{0,4},{1,5},{2,6},{3,7},{8,12},{9,13},{10,14},{11,15},{16,20},{17,... | collective-permute-start | bytes 110600 | tf_op jit(solution)/shard_map/while/body/eval_jaxpr/ppermute | solution.py:17
  555.9 19.5 %copy-start.85 = (f32[384]{0:T(512)S(1)}, f32[384]{0:T(512)}, u32[]{:S(2)}) copy-start(f32[384]{0:T(512)} %get-tuple-element.1766) | copy-start | bytes 4612 | tf_op jit(solution)/shard_map/while
  555.9 19.7 %copy-start.27 = (f32[49,384]{1,0:T(8,128)S(1)}, f32[49,384]{1,0:T(8,128)}, u32[]{:S(2)}) copy-start(f32[49,384]{1,0:T(8,128)} %get-tuple-element.1895) | copy-start | bytes 225796 | tf_op jit(solution)/shard_map/while
  561.0 14.7 %collective-permute-start.5 = (bf16[24,16,384]{2,1,0:T(8,128)(2,1)S(1)}, bf16[24,16,384]{2,1,0:T(8,128)(2,1)S(1)}, u32[]{:S(2)}, u32[]{:S(2)}) collective-permute-start(bf16[24,16,384]{2,1,0:T(8,128)(2,1)S(1)} %fusion.416), channel_id=1, source_target_pairs={{8,0},{16,8},{24,16},{9,1},{17,9},{25,17},{10,2},{18,10},{26,18},{... | collective-permute-start | bytes 884744 | tf_op jit(solution)/shard_map/while/body/eval_jaxpr/ppermute | solution.py:28
  (459 other events, 1892.6 us)
Sparse Core Ops, SparseCore 0:
  576.5 119.0 all-reduce.6
where the time goes:
time: 716 us; the launch traced here: 707 us
  local copies, waits for them, and re-layouts  217 us (30%)
  other arithmetic  176 us (25%)
  waiting for transfers between devices  100 us (14%)
  starting transfers between devices  81.2 us (11%)
  matrix products  55.4 us (8%)
  loops' own time  34.7 us (5%)
  blocking collectives  28.8 us (4%)
  between operations  14.1 us (2%)
    psum x1, waiting for transfers between devices, body(): lax.psum((totals[0], totals[1], totals[2], totals[3], totals[4], totals[5...  88 us
    another operation x250, local copies, waits for them, and re-layouts, block_backward_second(): return (grad_in, jnp.stack(taps))  58.2 us
    ppermute x10, starting transfers between devices, extended(): lax.ppermute(lax.slice_in_dim(block, block.shape[dim] - width, None, axis...  36.3 us
    while x940, local copies, waits for them, and re-layouts  32.4 us
    ppermute x10, starting transfers between devices, shifted(): lax.ppermute(value, axis, [(source, source + steps) for source in range(l...  32 us
    psum x1, blocking collectives, body(): lax.psum((totals[0], totals[1], totals[2], totals[3], totals[4], totals[5...  28.8 us
    reduce_sum x5, other arithmetic, block_forward(): centred = conv - jnp.mean(conv, axis=-1, keepdims=True)  27 us
    reduce_sum x15, other arithmetic, block_backward_second(): jnp.sum(field[i:i + row_count, j:j + col_count] * grad_conv, axis=(0, 1))  26.8 us
  transfers between devices with their start and end apart: 31, of which 6 were waited for; matrix products, arithmetic and copies ran while one was open for 29% of the time, Pallas kernels for 0%

commit v1 on v0

--- a/solution.py
+++ b/solution.py
@@ -216,8 +216,10 @@
         lax.axis_size("dp") * slot_count * lax.axis_size("rows") * row_count * col_count
     )
     summed = lax.psum(
-        (totals[0], totals[1], totals[2], totals[3], totals[4], totals[5], totals[6]),
-        ("rows", "dp"),
+        lax.psum(
+            (totals[0], totals[1], totals[2], totals[3], totals[4], totals[5], totals[6]), "dp"
+        ),
+        "rows",
     )
     finished = tuple(((part * factor).astype(jnp.bfloat16) for part in summed))
     return (

time: 716 us -> 813 us (1.14)
  waiting for transfers between devices: 100 us -> 206 us
  blocking collectives: 28.8 us -> 19.5 us
    psum x1, waiting for transfers between devices: 88 us -> 184 us  [body(): lax.psum((totals[0], totals[1], totals[2], totals[3], totals[4], totals[5...]
    psum x1, blocking collectives: 28.8 us -> 16.2 us  [body(): lax.psum((totals[0], totals[1], totals[2], totals[3], totals[4], totals[5...]
    psum x0 -> x1, waiting for transfers between devices: none -> 9.32 us  [body(): lax.psum(lax.psum((totals[0], totals[1], totals[2], totals[3], totals[4],...]
  transfers between devices with their start and end apart: 31 -> 32, of which waited for: 6 -> 7; matrix products, arithmetic and copies ran while one was open for 29% -> 26% of each run, Pallas kernels for 0% -> 0%
where the time goes in v1:
time: 813 us; the launch traced here: 804 us
  local copies, waits for them, and re-layouts  217 us (27%)
  waiting for transfers between devices  206 us (25%)
  other arithmetic  176 us (22%)
  starting transfers between devices  81.3 us (10%)
  matrix products  55.4 us (7%)
  loops' own time  34.7 us (4%)
  blocking collectives  19.5 us (2%)
  between operations  14.1 us (2%)
    psum x1, waiting for transfers between devices, body(): lax.psum((totals[0], totals[1], totals[2], totals[3], totals[4], totals[5...  184 us
    another operation x250, local copies, waits for them, and re-layouts, block_backward_second(): return (grad_in, jnp.stack(taps))  58.2 us
    ppermute x10, starting transfers between devices, extended(): lax.ppermute(lax.slice_in_dim(block, block.shape[dim] - width, None, axis...  36.3 us
    while x940, local copies, waits for them, and re-layouts  32.4 us
    ppermute x10, starting transfers between devices, shifted(): lax.ppermute(value, axis, [(source, source + steps) for source in range(l...  32 us
    reduce_sum x5, other arithmetic, block_forward(): centred = conv - jnp.mean(conv, axis=-1, keepdims=True)  27 us
    reduce_sum x15, other arithmetic, block_backward_second(): jnp.sum(field[i:i + row_count, j:j + col_count] * grad_conv, axis=(0, 1))  26.8 us
    convert_element_type x5, other arithmetic, block_backward_second(): grad_in = (row_mask * (grad_res + total)).astype(jnp.bfloat16)  25.2 us
  transfers between devices with their start and end apart: 32, of which 7 were waited for; matrix products, arithmetic and copies ran while one was open for 26% of the time, Pallas kernels for 0%

profile of v1, /device:TPU:0, one launch (start us, length us, event | category | flops | bytes accessed | tf_op | source)
XLA Modules:
  0.0 803.8 jit_solution(6374721394736260511)
XLA Ops:
  10.1 2.7 broadcast_in_dim.122
  17.4 230.1 %while.58 = (s32[]{:T(128)}, bf16[24,16,384]{2,1,0:T(8,128)(2,1)S(1)}, bf16[2,30,16,384]{3,2,1,0:T(8,128)(2,1)}, f32[2,24,16,384]{3,2,1,0:T(8,128)}, f32[2,24,16...) while((s32[]{:T(128)}, ...), condition=%wide.region_5.6_spmd.clone, body=%wide.region_0.5_spmd.clone.sunk | while | flops 930707456 | bytes 118534944 | solution.py:184
  26.7 3.0 collective-permute-start.1
  42.0 5.4 fusion.394
  52.5 5.1 collective-permute-start.2
  61.0 2.4 collective-permute-done.2
  72.7 3.0 collective-permute-start.1
  88.0 5.4 fusion.394
  98.6 4.7 collective-permute-start.2
  118.3 3.0 collective-permute-start.1
  133.6 5.4 fusion.394
  144.2 4.7 collective-permute-start.2
  163.9 3.0 collective-permute-start.1
  179.2 5.4 fusion.394
  189.8 5.5 collective-permute-start.2
  198.6 2.4 collective-permute-done.2
  210.3 3.0 collective-permute-start.1
  225.6 5.4 fusion.394
  236.1 5.6 collective-permute-start.2
  245.1 2.4 collective-permute-done.2
  248.1 328.2 %while.59 = (s32[]{:T(128)}, bf16[24,16,384]{2,1,0:T(8,128)(2,1)S(1)}, f32[49,384]{1,0:T(8,128)}, f32[3,384]{1,0:T(4,128)}, f32[1,384]{1,0:T(1,128)}, /*index=5*...) while((s32[]{:T(128)}, ...), condition=%wide.region_64.65_spmd.clone, body=%wide.region_6.64_spmd.clone.sunk | while | flops 1859761920 | bytes 116535416 | solution.py:214
  258.3 3.3 fusion.410
  272.6 4.2 collective-permute-start.4
  285.7 3.4 fusion.423
  293.4 5.0 fusion.416
  323.0 3.3 fusion.410
  330.1 2.4 fusion.413
  337.3 4.2 collective-permute-start.4
  350.5 3.4 fusion.423
  358.2 5.0 fusion.416
  388.5 3.3 fusion.410
  395.6 2.4 fusion.413
  402.8 4.2 collective-permute-start.4
  416.0 3.4 fusion.423
  423.7 5.0 fusion.416
  454.0 3.3 fusion.410
  468.3 4.2 collective-permute-start.4
  482.1 3.4 fusion.423
  489.8 5.0 fusion.416
  520.1 3.3 fusion.410
  534.4 4.2 collective-permute-start.4
  548.2 3.4 fusion.423
  555.9 5.0 fusion.416
  576.4 184.4 %all-reduce.10.cloned.1.call-done = (f32[49,384]{1,0:T(8,128)}, f32[384,1536]{1,0:T(8,128)}, f32[1536,384]{1,0:T(8,128)}) async-done(((f32[49,384]{1,0:T(8,128)}, f32[384,1536]{1,0:T(8,128)}, f32[1536,384]{1,0:T(8,128)}), (f32[49,384]{1,0:T(8,128)}, f32[384,1536]{1,0:T(8,128)}, f32[1536,384]{1,0:T(8,128)})) %all-reduce.10.cloned.1.call-update) | async-done | bytes 4793872 | tf_op jit(solution)/shard_map/psum | solution.py:219
  761.5 16.2 %all-reduce.3 = (f32[3,384]{1,0:T(4,128)S(1)}, f32[1,384]{1,0:T(1,128)S(1)}, f32[1,384]{1,0:T(1,128)S(1)}, f32[1,1536]{1,0:T(1,128)S(1)}) all-reduce(f32[3,384]{1,0:T(4,128)S(1)} %copy-done.39, f32[1,384]{1,0:T(1,128)S(1)} %copy-done.90, f32[1,384]{1,0:T(1,128)S(1)} %copy-done.91, ...), channel_id=1, replica_groups=mesh['section'=4,'rows'=2,'dp'=4] {'dp'}, use_global_device_ids=true, to_apply=%region_67.68 | all-reduce | flops 3456 | bytes 27648 | tf_op jit(solution)/shard_map/psum | solution.py:219
  777.7 3.3 all-reduce.5
  782.8 9.3 %all-reduce.12.cloned.1.call-done = (f32[49,384]{1,0:T(8,128)}, f32[384,1536]{1,0:T(8,128)}, f32[1536,384]{1,0:T(8,128)}) async-done(((f32[49,384]{1,0:T(8,128)}, f32[384,1536]{1,0:T(8,128)}, f32[1536,384]{1,0:T(8,128)}), (f32[49,384]{1,0:T(8,128)}, f32[384,1536]{1,0:T(8,128)}, f32[1536,384]{1,0:T(8,128)})) %all-reduce.12.cloned.1.call-update) | async-done | bytes 4793872 | tf_op jit(solution)/shard_map/psum | solution.py:218
  792.1 3.0 fusion.334
  (1604 shorter events, 376.2 us)
Async XLA Ops:
  7.2 753.6 %all-reduce.10.cloned.1.call-start = ((), (), s32[]{:S(2)}) async-start(), calls=%async_computation | async-start | bytes 9609216 | tf_op jit(solution)/shard_map/psum | solution.py:219
  25.4 16.5 %collective-permute-start = (bf16[3,16,384]{2,1,0:T(8,128)(2,1)S(1)}, bf16[3,16,384]{2,1,0:T(8,128)(2,1)S(1)}, u32[]{:S(2)}, u32[]{:S(2)}) collective-permute-start(bf16[3,16,384]{2,1,0:T(8,128)(2,1)S(1)} %get-tuple-element.1580), channel_id=1, source_target_pairs={{4,0},{5,1},{6,2},{7,3},{12,8},{13,9},{14,10},{15,11},{20,16},{21,... | collective-permute-start | bytes 110600 | tf_op jit(solution)/shard_map/while/body/eval_jaxpr/ppermute | solution.py:20
  26.7 15.2 %collective-permute-start.1 = (bf16[3,16,384]{2,1,0:T(8,128)(2,1)S(1)}, bf16[3,16,384]{2,1,0:T(8,128)(2,1)S(1)}, u32[]{:S(2)}, u32[]{:S(2)}) collective-permute-start(bf16[3,16,384]{2,1,0:T(8,128)(2,1)S(1)} %get-tuple-element.1581), channel_id=1, source_target_pairs={{0,4},{1,5},{2,6},{3,7},{8,12},{9,13},{10,14},{11,15},{16,20},{17,... | collective-permute-start | bytes 110600 | tf_op jit(solution)/shard_map/while/body/eval_jaxpr/ppermute | solution.py:17
  52.5 10.9 %collective-permute-start.2 = (bf16[24,16,384]{2,1,0:T(8,128)(2,1)S(1)}, bf16[24,16,384]{2,1,0:T(8,128)(2,1)S(1)}, u32[]{:S(2)}, u32[]{:S(2)}) collective-permute-start(bf16[24,16,384]{2,1,0:T(8,128)(2,1)S(1)} %multiply_convert_fusion.15), channel_id=1, source_target_pairs={{0,8},{8,16},{16,24},{1,9},{9,17},{17,25},{2,10},{10,18},{18,26},{... | collective-permute-start | bytes 884744 | tf_op jit(solution)/shard_map/while/body/eval_jaxpr/ppermute | solution.py:28
  71.4 16.5 %collective-permute-start = (bf16[3,16,384]{2,1,0:T(8,128)(2,1)S(1)}, bf16[3,16,384]{2,1,0:T(8,128)(2,1)S(1)}, u32[]{:S(2)}, u32[]{:S(2)}) collective-permute-start(bf16[3,16,384]{2,1,0:T(8,128)(2,1)S(1)} %get-tuple-element.1580), channel_id=1, source_target_pairs={{4,0},{5,1},{6,2},{7,3},{12,8},{13,9},{14,10},{15,11},{20,16},{21,... | collective-permute-start | bytes 110600 | tf_op jit(solution)/shard_map/while/body/eval_jaxpr/ppermute | solution.py:20
  72.7 15.2 %collective-permute-start.1 = (bf16[3,16,384]{2,1,0:T(8,128)(2,1)S(1)}, bf16[3,16,384]{2,1,0:T(8,128)(2,1)S(1)}, u32[]{:S(2)}, u32[]{:S(2)}) collective-permute-start(bf16[3,16,384]{2,1,0:T(8,128)(2,1)S(1)} %get-tuple-element.1581), channel_id=1, source_target_pairs={{0,4},{1,5},{2,6},{3,7},{8,12},{9,13},{10,14},{11,15},{16,20},{17,... | collective-permute-start | bytes 110600 | tf_op jit(solution)/shard_map/while/body/eval_jaxpr/ppermute | solution.py:17
  98.6 10.5 %collective-permute-start.2 = (bf16[24,16,384]{2,1,0:T(8,128)(2,1)S(1)}, bf16[24,16,384]{2,1,0:T(8,128)(2,1)S(1)}, u32[]{:S(2)}, u32[]{:S(2)}) collective-permute-start(bf16[24,16,384]{2,1,0:T(8,128)(2,1)S(1)} %multiply_convert_fusion.15), channel_id=1, source_target_pairs={{0,8},{8,16},{16,24},{1,9},{9,17},{17,25},{2,10},{10,18},{18,26},{... | collective-permute-start | bytes 884744 | tf_op jit(solution)/shard_map/while/body/eval_jaxpr/ppermute | solution.py:28
  117.0 16.5 %collective-permute-start = (bf16[3,16,384]{2,1,0:T(8,128)(2,1)S(1)}, bf16[3,16,384]{2,1,0:T(8,128)(2,1)S(1)}, u32[]{:S(2)}, u32[]{:S(2)}) collective-permute-start(bf16[3,16,384]{2,1,0:T(8,128)(2,1)S(1)} %get-tuple-element.1580), channel_id=1, source_target_pairs={{4,0},{5,1},{6,2},{7,3},{12,8},{13,9},{14,10},{15,11},{20,16},{21,... | collective-permute-start | bytes 110600 | tf_op jit(solution)/shard_map/while/body/eval_jaxpr/ppermute | solution.py:20
  118.3 15.2 %collective-permute-start.1 = (bf16[3,16,384]{2,1,0:T(8,128)(2,1)S(1)}, bf16[3,16,384]{2,1,0:T(8,128)(2,1)S(1)}, u32[]{:S(2)}, u32[]{:S(2)}) collective-permute-start(bf16[3,16,384]{2,1,0:T(8,128)(2,1)S(1)} %get-tuple-element.1581), channel_id=1, source_target_pairs={{0,4},{1,5},{2,6},{3,7},{8,12},{9,13},{10,14},{11,15},{16,20},{17,... | collective-permute-start | bytes 110600 | tf_op jit(solution)/shard_map/while/body/eval_jaxpr/ppermute | solution.py:17
  144.2 10.5 %collective-permute-start.2 = (bf16[24,16,384]{2,1,0:T(8,128)(2,1)S(1)}, bf16[24,16,384]{2,1,0:T(8,128)(2,1)S(1)}, u32[]{:S(2)}, u32[]{:S(2)}) collective-permute-start(bf16[24,16,384]{2,1,0:T(8,128)(2,1)S(1)} %multiply_convert_fusion.15), channel_id=1, source_target_pairs={{0,8},{8,16},{16,24},{1,9},{9,17},{17,25},{2,10},{10,18},{18,26},{... | collective-permute-start | bytes 884744 | tf_op jit(solution)/shard_map/while/body/eval_jaxpr/ppermute | solution.py:28
  162.6 16.5 %collective-permute-start = (bf16[3,16,384]{2,1,0:T(8,128)(2,1)S(1)}, bf16[3,16,384]{2,1,0:T(8,128)(2,1)S(1)}, u32[]{:S(2)}, u32[]{:S(2)}) collective-permute-start(bf16[3,16,384]{2,1,0:T(8,128)(2,1)S(1)} %get-tuple-element.1580), channel_id=1, source_target_pairs={{4,0},{5,1},{6,2},{7,3},{12,8},{13,9},{14,10},{15,11},{20,16},{21,... | collective-permute-start | bytes 110600 | tf_op jit(solution)/shard_map/while/body/eval_jaxpr/ppermute | solution.py:20
  163.9 15.2 %collective-permute-start.1 = (bf16[3,16,384]{2,1,0:T(8,128)(2,1)S(1)}, bf16[3,16,384]{2,1,0:T(8,128)(2,1)S(1)}, u32[]{:S(2)}, u32[]{:S(2)}) collective-permute-start(bf16[3,16,384]{2,1,0:T(8,128)(2,1)S(1)} %get-tuple-element.1581), channel_id=1, source_target_pairs={{0,4},{1,5},{2,6},{3,7},{8,12},{9,13},{10,14},{11,15},{16,20},{17,... | collective-permute-start | bytes 110600 | tf_op jit(solution)/shard_map/while/body/eval_jaxpr/ppermute | solution.py:17
  189.8 11.3 %collective-permute-start.2 = (bf16[24,16,384]{2,1,0:T(8,128)(2,1)S(1)}, bf16[24,16,384]{2,1,0:T(8,128)(2,1)S(1)}, u32[]{:S(2)}, u32[]{:S(2)}) collective-permute-start(bf16[24,16,384]{2,1,0:T(8,128)(2,1)S(1)} %multiply_convert_fusion.15), channel_id=1, source_target_pairs={{0,8},{8,16},{16,24},{1,9},{9,17},{17,25},{2,10},{10,18},{18,26},{... | collective-permute-start | bytes 884744 | tf_op jit(solution)/shard_map/while/body/eval_jaxpr/ppermute | solution.py:28
  209.0 16.5 %collective-permute-start = (bf16[3,16,384]{2,1,0:T(8,128)(2,1)S(1)}, bf16[3,16,384]{2,1,0:T(8,128)(2,1)S(1)}, u32[]{:S(2)}, u32[]{:S(2)}) collective-permute-start(bf16[3,16,384]{2,1,0:T(8,128)(2,1)S(1)} %get-tuple-element.1580), channel_id=1, source_target_pairs={{4,0},{5,1},{6,2},{7,3},{12,8},{13,9},{14,10},{15,11},{20,16},{21,... | collective-permute-start | bytes 110600 | tf_op jit(solution)/shard_map/while/body/eval_jaxpr/ppermute | solution.py:20
  210.3 15.2 %collective-permute-start.1 = (bf16[3,16,384]{2,1,0:T(8,128)(2,1)S(1)}, bf16[3,16,384]{2,1,0:T(8,128)(2,1)S(1)}, u32[]{:S(2)}, u32[]{:S(2)}) collective-permute-start(bf16[3,16,384]{2,1,0:T(8,128)(2,1)S(1)} %get-tuple-element.1581), channel_id=1, source_target_pairs={{0,4},{1,5},{2,6},{3,7},{8,12},{9,13},{10,14},{11,15},{16,20},{17,... | collective-permute-start | bytes 110600 | tf_op jit(solution)/shard_map/while/body/eval_jaxpr/ppermute | solution.py:17
  236.1 11.4 %collective-permute-start.2 = (bf16[24,16,384]{2,1,0:T(8,128)(2,1)S(1)}, bf16[24,16,384]{2,1,0:T(8,128)(2,1)S(1)}, u32[]{:S(2)}, u32[]{:S(2)}) collective-permute-start(bf16[24,16,384]{2,1,0:T(8,128)(2,1)S(1)} %multiply_convert_fusion.15), channel_id=1, source_target_pairs={{0,8},{8,16},{16,24},{1,9},{9,17},{17,25},{2,10},{10,18},{18,26},{... | collective-permute-start | bytes 884744 | tf_op jit(solution)/shard_map/while/body/eval_jaxpr/ppermute | solution.py:28
  248.3 9.9 %copy-start.87 = (f32[1,384]{1,0:T(1,128)S(1)}, f32[1,384]{1,0:T(1,128)}, u32[]{:S(2)}) copy-start(f32[1,384]{1,0:T(1,128)} %get-tuple-element.1952) | copy-start | bytes 4612 | tf_op jit(solution)/shard_map/while
  248.3 9.9 %copy-start.97 = (bf16[1536,384]{1,0:T(8,128)(2,1)S(1)}, bf16[1536,384]{1,0:T(8,128)(2,1)}, u32[]{:S(2)}) copy-start(bf16[1536,384]{1,0:T(8,128)(2,1)} %get-tuple-element.1949) | copy-start | bytes 3538948 | tf_op jit(solution)/shard_map/while
  271.3 20.9 %collective-permute-start.3 = (bf16[3,16,384]{2,1,0:T(8,128)(2,1)}, bf16[3,16,384]{2,1,0:T(8,128)(2,1)}, u32[]{:S(2)}, u32[]{:S(2)}) collective-permute-start(bf16[3,16,384]{2,1,0:T(8,128)(2,1)} %get-tuple-element.1673), channel_id=1, source_target_pairs={{4,0},{5,1},{6,2},{7,3},{12,8},{13,9},{14,10},{15,11},{20,16},{21,... | collective-permute-start | bytes 110600 | tf_op jit(solution)/shard_map/while/body/eval_jaxpr/ppermute | solution.py:20
  272.6 19.6 %collective-permute-start.4 = (bf16[3,16,384]{2,1,0:T(8,128)(2,1)}, bf16[3,16,384]{2,1,0:T(8,128)(2,1)}, u32[]{:S(2)}, u32[]{:S(2)}) collective-permute-start(bf16[3,16,384]{2,1,0:T(8,128)(2,1)} %get-tuple-element.1674), channel_id=1, source_target_pairs={{0,4},{1,5},{2,6},{3,7},{8,12},{9,13},{10,14},{11,15},{16,20},{17,... | collective-permute-start | bytes 110600 | tf_op jit(solution)/shard_map/while/body/eval_jaxpr/ppermute | solution.py:17
  293.4 18.8 %copy-start.85 = (f32[384]{0:T(512)S(1)}, f32[384]{0:T(512)}, u32[]{:S(2)}) copy-start(f32[384]{0:T(512)} %get-tuple-element.1773) | copy-start | bytes 4612 | tf_op jit(solution)/shard_map/while
  293.4 19.0 %copy-start.27 = (f32[49,384]{1,0:T(8,128)S(1)}, f32[49,384]{1,0:T(8,128)}, u32[]{:S(2)}) copy-start(f32[49,384]{1,0:T(8,128)} %get-tuple-element.1902) | copy-start | bytes 225796 | tf_op jit(solution)/shard_map/while
  298.5 14.0 %collective-permute-start.5 = (bf16[24,16,384]{2,1,0:T(8,128)(2,1)S(1)}, bf16[24,16,384]{2,1,0:T(8,128)(2,1)S(1)}, u32[]{:S(2)}, u32[]{:S(2)}) collective-permute-start(bf16[24,16,384]{2,1,0:T(8,128)(2,1)S(1)} %fusion.416), channel_id=1, source_target_pairs={{8,0},{16,8},{24,16},{9,1},{17,9},{25,17},{10,2},{18,10},{26,18},{... | collective-permute-start | bytes 884744 | tf_op jit(solution)/shard_map/while/body/eval_jaxpr/ppermute | solution.py:28
  313.1 9.9 %copy-start.97 = (bf16[1536,384]{1,0:T(8,128)(2,1)S(1)}, bf16[1536,384]{1,0:T(8,128)(2,1)}, u32[]{:S(2)}) copy-start(bf16[1536,384]{1,0:T(8,128)(2,1)} %get-tuple-element.1949) | copy-start | bytes 3538948 | tf_op jit(solution)/shard_map/while
  336.1 20.9 %collective-permute-start.3 = (bf16[3,16,384]{2,1,0:T(8,128)(2,1)}, bf16[3,16,384]{2,1,0:T(8,128)(2,1)}, u32[]{:S(2)}, u32[]{:S(2)}) collective-permute-start(bf16[3,16,384]{2,1,0:T(8,128)(2,1)} %get-tuple-element.1673), channel_id=1, source_target_pairs={{4,0},{5,1},{6,2},{7,3},{12,8},{13,9},{14,10},{15,11},{20,16},{21,... | collective-permute-start | bytes 110600 | tf_op jit(solution)/shard_map/while/body/eval_jaxpr/ppermute | solution.py:20
  337.3 19.6 %collective-permute-start.4 = (bf16[3,16,384]{2,1,0:T(8,128)(2,1)}, bf16[3,16,384]{2,1,0:T(8,128)(2,1)}, u32[]{:S(2)}, u32[]{:S(2)}) collective-permute-start(bf16[3,16,384]{2,1,0:T(8,128)(2,1)} %get-tuple-element.1674), channel_id=1, source_target_pairs={{0,4},{1,5},{2,6},{3,7},{8,12},{9,13},{10,14},{11,15},{16,20},{17,... | collective-permute-start | bytes 110600 | tf_op jit(solution)/shard_map/while/body/eval_jaxpr/ppermute | solution.py:17
  358.2 19.5 %copy-start.85 = (f32[384]{0:T(512)S(1)}, f32[384]{0:T(512)}, u32[]{:S(2)}) copy-start(f32[384]{0:T(512)} %get-tuple-element.1773) | copy-start | bytes 4612 | tf_op jit(solution)/shard_map/while
  358.2 19.7 %copy-start.27 = (f32[49,384]{1,0:T(8,128)S(1)}, f32[49,384]{1,0:T(8,128)}, u32[]{:S(2)}) copy-start(f32[49,384]{1,0:T(8,128)} %get-tuple-element.1902) | copy-start | bytes 225796 | tf_op jit(solution)/shard_map/while
  363.3 14.7 %collective-permute-start.5 = (bf16[24,16,384]{2,1,0:T(8,128)(2,1)S(1)}, bf16[24,16,384]{2,1,0:T(8,128)(2,1)S(1)}, u32[]{:S(2)}, u32[]{:S(2)}) collective-permute-start(bf16[24,16,384]{2,1,0:T(8,128)(2,1)S(1)} %fusion.416), channel_id=1, source_target_pairs={{8,0},{16,8},{24,16},{9,1},{17,9},{25,17},{10,2},{18,10},{26,18},{... | collective-permute-start | bytes 884744 | tf_op jit(solution)/shard_map/while/body/eval_jaxpr/ppermute | solution.py:28
  378.6 9.9 %copy-start.97 = (bf16[1536,384]{1,0:T(8,128)(2,1)S(1)}, bf16[1536,384]{1,0:T(8,128)(2,1)}, u32[]{:S(2)}) copy-start(bf16[1536,384]{1,0:T(8,128)(2,1)} %get-tuple-element.1949) | copy-start | bytes 3538948 | tf_op jit(solution)/shard_map/while
  401.5 20.9 %collective-permute-start.3 = (bf16[3,16,384]{2,1,0:T(8,128)(2,1)}, bf16[3,16,384]{2,1,0:T(8,128)(2,1)}, u32[]{:S(2)}, u32[]{:S(2)}) collective-permute-start(bf16[3,16,384]{2,1,0:T(8,128)(2,1)} %get-tuple-element.1673), channel_id=1, source_target_pairs={{4,0},{5,1},{6,2},{7,3},{12,8},{13,9},{14,10},{15,11},{20,16},{21,... | collective-permute-start | bytes 110600 | tf_op jit(solution)/shard_map/while/body/eval_jaxpr/ppermute | solution.py:20
  402.8 19.6 %collective-permute-start.4 = (bf16[3,16,384]{2,1,0:T(8,128)(2,1)}, bf16[3,16,384]{2,1,0:T(8,128)(2,1)}, u32[]{:S(2)}, u32[]{:S(2)}) collective-permute-start(bf16[3,16,384]{2,1,0:T(8,128)(2,1)} %get-tuple-element.1674), channel_id=1, source_target_pairs={{0,4},{1,5},{2,6},{3,7},{8,12},{9,13},{10,14},{11,15},{16,20},{17,... | collective-permute-start | bytes 110600 | tf_op jit(solution)/shard_map/while/body/eval_jaxpr/ppermute | solution.py:17
  423.7 19.5 %copy-start.85 = (f32[384]{0:T(512)S(1)}, f32[384]{0:T(512)}, u32[]{:S(2)}) copy-start(f32[384]{0:T(512)} %get-tuple-element.1773) | copy-start | bytes 4612 | tf_op jit(solution)/shard_map/while
  423.7 19.7 %copy-start.27 = (f32[49,384]{1,0:T(8,128)S(1)}, f32[49,384]{1,0:T(8,128)}, u32[]{:S(2)}) copy-start(f32[49,384]{1,0:T(8,128)} %get-tuple-element.1902) | copy-start | bytes 225796 | tf_op jit(solution)/shard_map/while
  428.7 14.7 %collective-permute-start.5 = (bf16[24,16,384]{2,1,0:T(8,128)(2,1)S(1)}, bf16[24,16,384]{2,1,0:T(8,128)(2,1)S(1)}, u32[]{:S(2)}, u32[]{:S(2)}) collective-permute-start(bf16[24,16,384]{2,1,0:T(8,128)(2,1)S(1)} %fusion.416), channel_id=1, source_target_pairs={{8,0},{16,8},{24,16},{9,1},{17,9},{25,17},{10,2},{18,10},{26,18},{... | collective-permute-start | bytes 884744 | tf_op jit(solution)/shard_map/while/body/eval_jaxpr/ppermute | solution.py:28
  444.1 9.9 %copy-start.97 = (bf16[1536,384]{1,0:T(8,128)(2,1)S(1)}, bf16[1536,384]{1,0:T(8,128)(2,1)}, u32[]{:S(2)}) copy-start(bf16[1536,384]{1,0:T(8,128)(2,1)} %get-tuple-element.1949) | copy-start | bytes 3538948 | tf_op jit(solution)/shard_map/while
  467.0 21.5 %collective-permute-start.3 = (bf16[3,16,384]{2,1,0:T(8,128)(2,1)}, bf16[3,16,384]{2,1,0:T(8,128)(2,1)}, u32[]{:S(2)}, u32[]{:S(2)}) collective-permute-start(bf16[3,16,384]{2,1,0:T(8,128)(2,1)} %get-tuple-element.1673), channel_id=1, source_target_pairs={{4,0},{5,1},{6,2},{7,3},{12,8},{13,9},{14,10},{15,11},{20,16},{21,... | collective-permute-start | bytes 110600 | tf_op jit(solution)/shard_map/while/body/eval_jaxpr/ppermute | solution.py:20
  468.3 20.2 %collective-permute-start.4 = (bf16[3,16,384]{2,1,0:T(8,128)(2,1)}, bf16[3,16,384]{2,1,0:T(8,128)(2,1)}, u32[]{:S(2)}, u32[]{:S(2)}) collective-permute-start(bf16[3,16,384]{2,1,0:T(8,128)(2,1)} %get-tuple-element.1674), channel_id=1, source_target_pairs={{0,4},{1,5},{2,6},{3,7},{8,12},{9,13},{10,14},{11,15},{16,20},{17,... | collective-permute-start | bytes 110600 | tf_op jit(solution)/shard_map/while/body/eval_jaxpr/ppermute | solution.py:17
  489.8 19.5 %copy-start.85 = (f32[384]{0:T(512)S(1)}, f32[384]{0:T(512)}, u32[]{:S(2)}) copy-start(f32[384]{0:T(512)} %get-tuple-element.1773) | copy-start | bytes 4612 | tf_op jit(solution)/shard_map/while
  489.8 19.7 %copy-start.27 = (f32[49,384]{1,0:T(8,128)S(1)}, f32[49,384]{1,0:T(8,128)}, u32[]{:S(2)}) copy-start(f32[49,384]{1,0:T(8,128)} %get-tuple-element.1902) | copy-start | bytes 225796 | tf_op jit(solution)/shard_map/while
  494.9 14.7 %collective-permute-start.5 = (bf16[24,16,384]{2,1,0:T(8,128)(2,1)S(1)}, bf16[24,16,384]{2,1,0:T(8,128)(2,1)S(1)}, u32[]{:S(2)}, u32[]{:S(2)}) collective-permute-start(bf16[24,16,384]{2,1,0:T(8,128)(2,1)S(1)} %fusion.416), channel_id=1, source_target_pairs={{8,0},{16,8},{24,16},{9,1},{17,9},{25,17},{10,2},{18,10},{26,18},{... | collective-permute-start | bytes 884744 | tf_op jit(solution)/shard_map/while/body/eval_jaxpr/ppermute | solution.py:28
  510.2 9.9 %copy-start.97 = (bf16[1536,384]{1,0:T(8,128)(2,1)S(1)}, bf16[1536,384]{1,0:T(8,128)(2,1)}, u32[]{:S(2)}) copy-start(bf16[1536,384]{1,0:T(8,128)(2,1)} %get-tuple-element.1949) | copy-start | bytes 3538948 | tf_op jit(solution)/shard_map/while
  533.1 21.5 %collective-permute-start.3 = (bf16[3,16,384]{2,1,0:T(8,128)(2,1)}, bf16[3,16,384]{2,1,0:T(8,128)(2,1)}, u32[]{:S(2)}, u32[]{:S(2)}) collective-permute-start(bf16[3,16,384]{2,1,0:T(8,128)(2,1)} %get-tuple-element.1673), channel_id=1, source_target_pairs={{4,0},{5,1},{6,2},{7,3},{12,8},{13,9},{14,10},{15,11},{20,16},{21,... | collective-permute-start | bytes 110600 | tf_op jit(solution)/shard_map/while/body/eval_jaxpr/ppermute | solution.py:20
  534.4 20.2 %collective-permute-start.4 = (bf16[3,16,384]{2,1,0:T(8,128)(2,1)}, bf16[3,16,384]{2,1,0:T(8,128)(2,1)}, u32[]{:S(2)}, u32[]{:S(2)}) collective-permute-start(bf16[3,16,384]{2,1,0:T(8,128)(2,1)} %get-tuple-element.1674), channel_id=1, source_target_pairs={{0,4},{1,5},{2,6},{3,7},{8,12},{9,13},{10,14},{11,15},{16,20},{17,... | collective-permute-start | bytes 110600 | tf_op jit(solution)/shard_map/while/body/eval_jaxpr/ppermute | solution.py:17
  555.9 19.5 %copy-start.85 = (f32[384]{0:T(512)S(1)}, f32[384]{0:T(512)}, u32[]{:S(2)}) copy-start(f32[384]{0:T(512)} %get-tuple-element.1773) | copy-start | bytes 4612 | tf_op jit(solution)/shard_map/while
  555.9 19.7 %copy-start.27 = (f32[49,384]{1,0:T(8,128)S(1)}, f32[49,384]{1,0:T(8,128)}, u32[]{:S(2)}) copy-start(f32[49,384]{1,0:T(8,128)} %get-tuple-element.1902) | copy-start | bytes 225796 | tf_op jit(solution)/shard_map/while
  561.0 14.7 %collective-permute-start.5 = (bf16[24,16,384]{2,1,0:T(8,128)(2,1)S(1)}, bf16[24,16,384]{2,1,0:T(8,128)(2,1)S(1)}, u32[]{:S(2)}, u32[]{:S(2)}) collective-permute-start(bf16[24,16,384]{2,1,0:T(8,128)(2,1)S(1)} %fusion.416), channel_id=1, source_target_pairs={{8,0},{16,8},{24,16},{9,1},{17,9},{25,17},{10,2},{18,10},{26,18},{... | collective-permute-start | bytes 884744 | tf_op jit(solution)/shard_map/while/body/eval_jaxpr/ppermute | solution.py:28
  576.3 215.8 %all-reduce.12.cloned.1.call-start = ((), (), s32[]{:S(2)}) async-start(), calls=%async_computation.1 | async-start | bytes 9609216 | tf_op jit(solution)/shard_map/psum | solution.py:218
  (460 other events, 1902.5 us)
Sparse Core Ops, SparseCore 0:
  576.4 184.2 all-reduce.9
  763.5 28.5 all-reduce.11
